TPU v7x, 32 devices: a whole 2x2x4 slice. The times are simulated.
32 devices in a mesh: blk: 8 (over z, y), grp: 4 (over x, core).
Axes of the slice: x: 2, y: 2, z: 4, core: 2. Of those that a mesh axis runs over, the one named last changes fastest.
Arguments:
- state: float32 [6, 131072], P(None, ('blk', 'grp')), may hold values from -6 to 6
- mass: float32 [131072], P(('blk', 'grp')), may hold values from 1.5258789e-06 to 3.8146973e-05
- active_index: int32 [8, 32], P('blk'), may hold values from 0 to 16383, as said below
- counts: int32 [8], P('blk'), may hold values from 8 to 32, as said below
Outputs:
- acc_jerk: float32 [6, 256], P(None, 'blk')
- potential: float32 [256], P('blk')
Inputs may be any that keep to these rules, and one draw needn't show every extreme that they name: `active_index`: each row holds 32 different star numbers of its slot block; only the first counts[b] entries of row b are active. `counts`: in every draw some slot is full, with 32 active stars.
All inputs are finite; a program needn't handle non-finite values.
Results may differ from a plain program's by a relative error of at most 0.0003.
Values sent between devices are 32-bit elements; how exact they have to be, the bound alone decides.
A program may use at most 64 MiB of HBM per device.

v0:
```python
import jax
import jax.numpy as jnp
from jax import lax
from jax.sharding import PartitionSpec as P

softening = 0.001


def shifted(block, axis, distance):
    devices = range(lax.axis_size(axis))
    route = [((i - distance) % len(devices), i) for i in devices]
    return lax.ppermute(block, axis, route)


def pair_terms(active, field):
    dpos = field[0:3, None, :] - active[0:3, :, None]
    dvel = field[3:6, None, :] - active[3:6, :, None]
    raw = jnp.sum(dpos * dpos, axis=0)
    weight = jnp.where(raw == 0.0, 0.0, field[6][None, :])
    inv = lax.rsqrt(raw + softening)
    first = weight * inv
    third = first * inv * inv
    along = jnp.sum(dpos * dvel, axis=0)
    fifth = 3.0 * along * third * inv * inv
    accel = jnp.sum(third[None] * dpos, axis=-1)
    jerk = jnp.sum(third[None] * dvel - fifth[None] * dpos, axis=-1)
    pot = -jnp.sum(first, axis=-1)
    return jnp.concatenate([accel, jerk, pot[None]], axis=0)


def live_terms(active, field):
    return pair_terms(active, field)


def on_device(state, mass, active_index, counts):
    blocks = lax.axis_size("blk")
    capacity = active_index.shape[1]
    picks = active_index[0]
    count_live = counts[0]
    slot_state = lax.all_gather(state, "grp", axis=1, tiled=True)
    active = jnp.take(slot_state, picks, axis=1)
    field = jnp.concatenate([state, mass[None, :]], axis=0)

    def turn_one(step, carry):
        summed, moving = carry
        moving = shifted(moving, "blk", 1)
        return (summed + live_terms(active, moving), moving)

    start = live_terms(active, field)
    total = lax.fori_loop(1, blocks, turn_one, (start, field))[0]
    live = jnp.arange(capacity, dtype=jnp.int32) < count_live
    total = jnp.where(live[None, :], total, 0.0)
    summed = lax.psum(total, "grp")
    return (summed[0:6], summed[6])


def solution(mesh):
    placed = (P(None, ("blk", "grp")), P(("blk", "grp")), P("blk", None), P("blk"))
    return jax.shard_map(
        on_device, mesh=mesh, in_specs=placed, out_specs=(P(None, "blk"), P("blk")), check_vma=False
    )
```

profile of v0, /device:TPU:0, one launch (start us, length us, event | category | flops | bytes accessed | tf_op | source)
XLA Modules:
  0.0 132.4 jit_solution(1626110730015682410)
XLA Ops:
  0.6 1.5 %copy.10 = f32[6,4096]{0,1:T(8,128)S(1)} copy(f32[6,4096]{1,0:T(8,128)} %param.6) | data formatting | bytes 196608 | tf_op args[0]
  2.2 52.0 %all_gather.3 = f32[6,16384]{0,1:T(8,128)} all-gather(f32[6,4096]{0,1:T(8,128)S(1)} %copy.10), channel_id=1, replica_groups=mesh['blk'=8,'grp'=4] {'grp'}, dimensions={1}, use_global_device_ids=true | all-gather | bytes 491520 | tf_op jit(solution)/shard_map/all_gather | solution.py:40
  54.3 4.0 %gather_fusion = f32[32,6]{1,0:T(8,128)S(1)} fusion(f32[6,16384]{0,1:T(8,128)} %all_gather.3, s32[1024]{0:T(1024)S(1)} %pad_clamp_fusion), kind=kCustom, calls=%fused_computation | custom fusion | bytes 1664 | tf_op jit(solution)/shard_map/jit(_take)/gather | solution.py:41
  58.6 0.4 fusion.10
  59.0 0.3 multiply_multiply_fusion.2
  59.3 0.6 fusion.9
  60.1 65.4 %while.12 = (s32[]{:T(128)}, f32[7,32]{1,0:T(8,128)S(1)}, f32[7,4096]{1,0:T(8,128)S(1)}, f32[6,32]{1,0:T(8,128)S(1)}, s32[]{:T(128)}) while((s32[]{:T(128)}, f32[7,32]{1,0:T(8,128)S(1)}, f32[7,4096]{1,0:T(8,128)S(1)}, f32[6,32]{1,0:T(8,128)S(1)}, s32[]{:T(128)}) %tuple.46), condition=%wide.region_11.12_spmd, body=%wide.region_5.11_spmd.sunk | while | flops 6685154 | bytes 5331813 | solution.py:50
  60.1 1.6 %collective-permute-start = (f32[7,4096]{1,0:T(8,128)S(1)}, f32[7,4096]{1,0:T(8,128)S(1)}, u32[]{:S(2)}, u32[]{:S(2)}) collective-permute-start(f32[7,4096]{1,0:T(8,128)S(1)} %get-tuple-element.117), channel_id=1, source_target_pairs={{28,0},{0,4},{4,8},{8,12},{12,16},{16,20},{20,24},{24,28},{29,1},{... | collective-permute-start | bytes 344072 | tf_op jit(solution)/shard_map/while/body/eval_jaxpr/ppermute | solution.py:12
  61.7 7.1 %collective-permute-done = f32[7,4096]{1,0:T(8,128)S(1)} collective-permute-done((f32[7,4096]{1,0:T(8,128)S(1)}, f32[7,4096]{1,0:T(8,128)S(1)}, u32[]{:S(2)}, u32[]{:S(2)}) %collective-permute-start) | collective-permute-done | bytes 114720 | tf_op jit(solution)/shard_map/while/body/eval_jaxpr/ppermute | solution.py:12
  68.8 0.4 fusion.23
  69.2 0.3 multiply_multiply_fusion.5
  69.5 0.6 fusion.24
  70.3 7.7 %collective-permute-done = f32[7,4096]{1,0:T(8,128)S(1)} collective-permute-done((f32[7,4096]{1,0:T(8,128)S(1)}, f32[7,4096]{1,0:T(8,128)S(1)}, u32[]{:S(2)}, u32[]{:S(2)}) %collective-permute-start) | collective-permute-done | bytes 114720 | tf_op jit(solution)/shard_map/while/body/eval_jaxpr/ppermute | solution.py:12
  78.0 0.4 fusion.23
  78.8 0.6 fusion.24
  79.6 7.6 %collective-permute-done = f32[7,4096]{1,0:T(8,128)S(1)} collective-permute-done((f32[7,4096]{1,0:T(8,128)S(1)}, f32[7,4096]{1,0:T(8,128)S(1)}, u32[]{:S(2)}, u32[]{:S(2)}) %collective-permute-start) | collective-permute-done | bytes 114720 | tf_op jit(solution)/shard_map/while/body/eval_jaxpr/ppermute | solution.py:12
  87.2 0.4 fusion.23
  88.0 0.6 fusion.24
  88.8 7.6 %collective-permute-done = f32[7,4096]{1,0:T(8,128)S(1)} collective-permute-done((f32[7,4096]{1,0:T(8,128)S(1)}, f32[7,4096]{1,0:T(8,128)S(1)}, u32[]{:S(2)}, u32[]{:S(2)}) %collective-permute-start) | collective-permute-done | bytes 114720 | tf_op jit(solution)/shard_map/while/body/eval_jaxpr/ppermute | solution.py:12
  96.4 0.4 fusion.23
  97.2 0.6 fusion.24
  97.9 7.6 %collective-permute-done = f32[7,4096]{1,0:T(8,128)S(1)} collective-permute-done((f32[7,4096]{1,0:T(8,128)S(1)}, f32[7,4096]{1,0:T(8,128)S(1)}, u32[]{:S(2)}, u32[]{:S(2)}) %collective-permute-start) | collective-permute-done | bytes 114720 | tf_op jit(solution)/shard_map/while/body/eval_jaxpr/ppermute | solution.py:12
  105.6 0.4 fusion.23
  106.4 0.6 fusion.24
  107.1 7.6 %collective-permute-done = f32[7,4096]{1,0:T(8,128)S(1)} collective-permute-done((f32[7,4096]{1,0:T(8,128)S(1)}, f32[7,4096]{1,0:T(8,128)S(1)}, u32[]{:S(2)}, u32[]{:S(2)}) %collective-permute-start) | collective-permute-done | bytes 114720 | tf_op jit(solution)/shard_map/while/body/eval_jaxpr/ppermute | solution.py:12
  114.8 0.4 fusion.23
  115.6 0.6 fusion.24
  116.3 7.6 %collective-permute-done = f32[7,4096]{1,0:T(8,128)S(1)} collective-permute-done((f32[7,4096]{1,0:T(8,128)S(1)}, f32[7,4096]{1,0:T(8,128)S(1)}, u32[]{:S(2)}, u32[]{:S(2)}) %collective-permute-start) | collective-permute-done | bytes 114720 | tf_op jit(solution)/shard_map/while/body/eval_jaxpr/ppermute | solution.py:12
  124.0 0.4 fusion.23
  124.8 0.6 fusion.24
  126.1 5.7 %psum.7 = f32[7,32]{1,0:T(8,128)S(1)} all-reduce(f32[7,32]{1,0:T(8,128)S(1)} %broadcast_select_fusion), channel_id=1, replica_groups=mesh['blk'=8,'grp'=4] {'grp'}, use_global_device_ids=true, to_apply=%region_12.13 | all-reduce | flops 224 | bytes 1792 | tf_op jit(solution)/shard_map/psum | solution.py:53
  131.8 0.5 slice_bitcast_fusion
  (76 shorter events, 3.4 us)
Async XLA Ops:
  2.2 52.1 %copy-start.3 = (s32[1,32]{1,0:T(1,128)S(1)}, s32[1,32]{1,0:T(1,128)}, u32[]{:S(2)}) copy-start(s32[1,32]{1,0:T(1,128)} %param.8) | copy-start | bytes 388
  2.2 56.3 %copy-start = (f32[6,4096]{1,0:T(8,128)S(1)}, f32[6,4096]{1,0:T(8,128)}, u32[]{:S(2)}) copy-start(f32[6,4096]{1,0:T(8,128)} %param.6) | copy-start | bytes 294916
  54.2 4.8 %copy-start.1 = (f32[4096]{0:T(1024)S(1)}, f32[4096]{0:T(1024)}, u32[]{:S(2)}) copy-start(f32[4096]{0:T(1024)} %param.7) | copy-start | bytes 49156
  60.1 8.6 %collective-permute-start = (f32[7,4096]{1,0:T(8,128)S(1)}, f32[7,4096]{1,0:T(8,128)S(1)}, u32[]{:S(2)}, u32[]{:S(2)}) collective-permute-start(f32[7,4096]{1,0:T(8,128)S(1)} %get-tuple-element.117), channel_id=1, source_target_pairs={{28,0},{0,4},{4,8},{8,12},{12,16},{16,20},{20,24},{24,28},{29,1},{... | collective-permute-start | bytes 344072 | tf_op jit(solution)/shard_map/while/body/eval_jaxpr/ppermute | solution.py:12
  70.2 7.8 %collective-permute-start = (f32[7,4096]{1,0:T(8,128)S(1)}, f32[7,4096]{1,0:T(8,128)S(1)}, u32[]{:S(2)}, u32[]{:S(2)}) collective-permute-start(f32[7,4096]{1,0:T(8,128)S(1)} %get-tuple-element.117), channel_id=1, source_target_pairs={{28,0},{0,4},{4,8},{8,12},{12,16},{16,20},{20,24},{24,28},{29,1},{... | collective-permute-start | bytes 344072 | tf_op jit(solution)/shard_map/while/body/eval_jaxpr/ppermute | solution.py:12
  79.5 7.7 %collective-permute-start = (f32[7,4096]{1,0:T(8,128)S(1)}, f32[7,4096]{1,0:T(8,128)S(1)}, u32[]{:S(2)}, u32[]{:S(2)}) collective-permute-start(f32[7,4096]{1,0:T(8,128)S(1)} %get-tuple-element.117), channel_id=1, source_target_pairs={{28,0},{0,4},{4,8},{8,12},{12,16},{16,20},{20,24},{24,28},{29,1},{... | collective-permute-start | bytes 344072 | tf_op jit(solution)/shard_map/while/body/eval_jaxpr/ppermute | solution.py:12
  88.7 7.7 %collective-permute-start = (f32[7,4096]{1,0:T(8,128)S(1)}, f32[7,4096]{1,0:T(8,128)S(1)}, u32[]{:S(2)}, u32[]{:S(2)}) collective-permute-start(f32[7,4096]{1,0:T(8,128)S(1)} %get-tuple-element.117), channel_id=1, source_target_pairs={{28,0},{0,4},{4,8},{8,12},{12,16},{16,20},{20,24},{24,28},{29,1},{... | collective-permute-start | bytes 344072 | tf_op jit(solution)/shard_map/while/body/eval_jaxpr/ppermute | solution.py:12
  97.9 7.7 %collective-permute-start = (f32[7,4096]{1,0:T(8,128)S(1)}, f32[7,4096]{1,0:T(8,128)S(1)}, u32[]{:S(2)}, u32[]{:S(2)}) collective-permute-start(f32[7,4096]{1,0:T(8,128)S(1)} %get-tuple-element.117), channel_id=1, source_target_pairs={{28,0},{0,4},{4,8},{8,12},{12,16},{16,20},{20,24},{24,28},{29,1},{... | collective-permute-start | bytes 344072 | tf_op jit(solution)/shard_map/while/body/eval_jaxpr/ppermute | solution.py:12
  107.1 7.7 %collective-permute-start = (f32[7,4096]{1,0:T(8,128)S(1)}, f32[7,4096]{1,0:T(8,128)S(1)}, u32[]{:S(2)}, u32[]{:S(2)}) collective-permute-start(f32[7,4096]{1,0:T(8,128)S(1)} %get-tuple-element.117), channel_id=1, source_target_pairs={{28,0},{0,4},{4,8},{8,12},{12,16},{16,20},{20,24},{24,28},{29,1},{... | collective-permute-start | bytes 344072 | tf_op jit(solution)/shard_map/while/body/eval_jaxpr/ppermute | solution.py:12
  116.3 7.7 %collective-permute-start = (f32[7,4096]{1,0:T(8,128)S(1)}, f32[7,4096]{1,0:T(8,128)S(1)}, u32[]{:S(2)}, u32[]{:S(2)}) collective-permute-start(f32[7,4096]{1,0:T(8,128)S(1)} %get-tuple-element.117), channel_id=1, source_target_pairs={{28,0},{0,4},{4,8},{8,12},{12,16},{16,20},{20,24},{24,28},{29,1},{... | collective-permute-start | bytes 344072 | tf_op jit(solution)/shard_map/while/body/eval_jaxpr/ppermute | solution.py:12
  131.8 0.6 copy-start.2
where the time goes:
time: 133 us; the launch traced here: 132 us
  blocking collectives  57.7 us (43%)
  waiting for transfers between devices  53 us (40%)
  other arithmetic  11.1 us (8%)
  local copies, waits for them, and re-layouts  6.87 us (5%)
  starting transfers between devices  1.92 us (1%)
  between operations  1.38 us (1%)
    ppermute x7, waiting for transfers between devices, shifted(): return lax.ppermute(block, axis, route)  53 us
    all_gather x1, blocking collectives, on_device(): slot_state = lax.all_gather(state, 'grp', axis=1, tiled=True)  52 us
    psum x1, blocking collectives, on_device(): summed = lax.psum(total, 'grp')  5.67 us
    reduce_sum x8, other arithmetic, pair_terms(): accel = jnp.sum(third[None] * dpos, axis=-1)  5.02 us
    gather x1, local copies, waits for them, and re-layouts, on_device(): active = jnp.take(slot_state, picks, axis=1)  3.96 us
    reduce_sum x8, other arithmetic, pair_terms(): along = jnp.sum(dpos * dvel, axis=0)  3.27 us
  transfers between devices with their start and end apart: 7, of which 7 were waited for; matrix products, arithmetic and copies ran while one was open for 0% of the time, Pallas kernels for 0%

commit v1 on v0

v1 whole, which is shorter than its diff:
```python
import functools

import jax
import jax.numpy as jnp
from jax import lax
from jax.experimental import pallas as pl
from jax.experimental.pallas import tpu as pltpu
from jax.sharding import PartitionSpec as P

softening = 0.001
LANES = 128
MESH = pl.DeviceIdType.MESH
UNROLL = 4


def spread_chunk(state_ref, mass_ref, wide_ref, chunk):
    start = pl.multiple_of(chunk * LANES, LANES)
    rows = jnp.concatenate(
        [state_ref[:, pl.ds(start, LANES)], mass_ref[pl.ds(chunk, 1), :], jnp.zeros((1, LANES), jnp.float32)], axis=0
    )
    columns = rows.T
    for c in range(7):
        wide_ref[c, pl.ds(start, LANES), :] = jnp.broadcast_to(columns[:, c : c + 1], (LANES, LANES))


def tile_terms(active, wide_ref, stars):
    mine = [jnp.broadcast_to(active[c : c + 1, :], (8, LANES)) for c in range(6)]

    def body(step, totals):
        totals = list(totals)
        for u in range(UNROLL):
            at = pl.ds(pl.multiple_of((step * UNROLL + u) * 8, 8), 8)
            dx = [wide_ref[c, at, :] - mine[c] for c in range(3)]
            dv = [wide_ref[c, at, :] - mine[c] for c in range(3, 6)]
            raw = dx[0] * dx[0] + dx[1] * dx[1] + dx[2] * dx[2]
            weight = jnp.where(raw == 0.0, 0.0, wide_ref[6, at, :])
            inv = lax.rsqrt(raw + softening)
            square = inv * inv
            first = weight * inv
            third = first * square
            along = dx[0] * dv[0] + dx[1] * dv[1] + dx[2] * dv[2]
            ratio = (3.0 * along) * square
            for c in range(3):
                totals[c] = totals[c] + third * dx[c]
                totals[3 + c] = totals[3 + c] + third * (dv[c] - ratio * dx[c])
            totals[6] = totals[6] + first
        return tuple(totals)

    zero = jnp.zeros((8, LANES), jnp.float32)
    totals = lax.fori_loop(0, stars // (8 * UNROLL), body, (zero,) * 7)
    sums = [jnp.sum(t, axis=0, keepdims=True) for t in totals]
    return jnp.concatenate(sums[:6] + [-sums[6], jnp.zeros((1, LANES), jnp.float32)], axis=0)


def kernel(
    n_blk, n_grp, cap, state_ref, mass_ref, picks_ref, counts_ref, out_ref, pot_ref,
    wide_ref, part_ref, part_in, own_ref, own_in, sum_ref, sum_in, tot_ref, tot_in,
    part_s, part_r, own_s, own_r, sum_s, sum_r, tot_s, tot_r,
):
    blk, grp = lax.axis_index("blk"), lax.axis_index("grp")
    stars = state_ref.shape[1]
    size = LANES // cap
    tiles = n_blk // size
    tile, place = blk // size, blk % size
    hops = [(dt, dr) for dt in range(tiles) for dr in range(size)]

    def slot(dt, dr):
        return ((tile + dt) % tiles) * size + (place + dr) % size

    barrier = pltpu.get_barrier_semaphore()
    for d in range(1, n_grp):
        pl.semaphore_signal(barrier, inc=1, device_id=(blk, (grp + d) % n_grp), device_id_type=MESH)
    for dt, dr in hops[1:]:
        pl.semaphore_signal(barrier, inc=1, device_id=(slot(dt, dr), grp), device_id_type=MESH)

    picks = jnp.concatenate([picks_ref[...] - grp * stars] * size, axis=1)
    lane = lax.broadcasted_iota(jnp.int32, (1, LANES), 1)
    picks = jnp.where(lane // cap == place, picks, -1)
    depth = 512
    row = lax.broadcasted_iota(jnp.int32, (depth, LANES), 0)
    found = jnp.zeros((6, LANES), jnp.float32)
    for k in range(stars // depth):
        hot = jnp.where(row + k * depth == picks, 1.0, 0.0).astype(jnp.bfloat16)
        rest = state_ref[:, k * depth : (k + 1) * depth]
        for _ in range(3):
            piece = rest.astype(jnp.bfloat16)
            rest = rest - piece.astype(jnp.float32)
            found = found + jnp.dot(piece, hot, preferred_element_type=jnp.float32)
    part_ref[...] = jnp.concatenate([found, jnp.zeros((2, LANES), jnp.float32)], axis=0)

    pl.semaphore_wait(barrier, n_grp - 1 + n_blk - 1)

    def grp_copy(src, dst, send, recv, d):
        return pltpu.make_async_remote_copy(
            src_ref=src, dst_ref=dst.at[d - 1], send_sem=send.at[d - 1], recv_sem=recv.at[d - 1],
            device_id=(blk, (grp + d) % n_grp), device_id_type=MESH,
        )

    parts = [grp_copy(part_ref, part_in, part_s, part_r, d) for d in range(1, n_grp)]
    for copy in parts:
        copy.start()

    chunks = stars // LANES

    @pl.loop(0, chunks // 2)
    def _(chunk):
        spread_chunk(state_ref, mass_ref, wide_ref, chunk)

    own = part_ref[...]
    for d, copy in enumerate(parts):
        copy.wait_recv()
        own = own + part_in[d]
    own_ref[...] = own

    shares = {}
    for dt, dr in hops[1:]:
        shares[dt, dr] = pltpu.make_async_remote_copy(
            src_ref=own_ref, dst_ref=own_in.at[dt * size + dr], send_sem=own_s.at[dt * size + dr],
            recv_sem=own_r.at[dt * size + dr], device_id=(slot(dt, dr), grp), device_id_type=MESH,
        )
        shares[dt, dr].start()

    @pl.loop(chunks // 2, chunks)
    def _(chunk):
        spread_chunk(state_ref, mass_ref, wide_ref, chunk)

    results = {}
    for dt in range(tiles):
        active = own if dt == 0 else None
        for dr in range(size):
            if (dt, dr) != (0, 0):
                shares[dt, dr].wait_recv()
                got = own_in[dt * size + dr]
                active = got if active is None else active + got
        terms = tile_terms(active, wide_ref, stars)
        sum_ref[dt] = terms
        for dr in range(size):
            if (dt, dr) != (0, 0):
                results[dt, dr] = pltpu.make_async_remote_copy(
                    src_ref=sum_ref.at[dt], dst_ref=sum_in.at[dt * size + dr], send_sem=sum_s.at[dt * size + dr],
                    recv_sem=sum_r.at[dt * size + dr], device_id=(slot(tiles - dt, dr), grp), device_id_type=MESH,
                )
                results[dt, dr].start()

    total = sum_ref[0]
    for dt, dr in hops[1:]:
        results[dt, dr].wait_recv()
        total = total + sum_in[dt * size + dr]
    tot_ref[...] = total
    totals = [grp_copy(tot_ref, tot_in, tot_s, tot_r, d) for d in range(1, n_grp)]
    for copy in totals:
        copy.start()
    for d, copy in enumerate(totals):
        copy.wait_recv()
        total = total + tot_in[d]

    total = pltpu.roll(total, ((size - place) % size) * cap, 1)
    total = jnp.where(lane < counts_ref[0], total, 0.0)
    out_ref[...] = total[0:6, 0:cap]
    pot_ref[...] = total[6:7, 0:cap]

    for copy in parts + list(shares.values()) + list(results.values()) + totals:
        copy.wait_send()


def solution(mesh):
    n_blk, n_grp = mesh.shape["blk"], mesh.shape["grp"]

    def on_device(state, mass, active_index, counts):
        stars, cap = state.shape[1], active_index.shape[1]
        f32 = jnp.float32
        tile = (8, LANES)
        sems = pltpu.SemaphoreType.DMA
        vmem = pl.BlockSpec(memory_space=pltpu.VMEM)
        out, pot = pl.pallas_call(
            functools.partial(kernel, n_blk, n_grp, cap),
            out_shape=(jax.ShapeDtypeStruct((6, cap), f32), jax.ShapeDtypeStruct((1, cap), f32)),
            in_specs=[vmem, vmem, vmem, pl.BlockSpec(memory_space=pltpu.SMEM)],
            out_specs=(vmem, vmem),
            scratch_shapes=[
                pltpu.VMEM((7, stars, LANES), f32),
                pltpu.VMEM(tile, f32),
                pltpu.VMEM((n_grp - 1, *tile), f32),
                pltpu.VMEM(tile, f32),
                pltpu.VMEM((n_blk, *tile), f32),
                pltpu.VMEM((n_blk * cap // LANES, *tile), f32),
                pltpu.VMEM((n_blk, *tile), f32),
                pltpu.VMEM(tile, f32),
                pltpu.VMEM((n_grp - 1, *tile), f32),
                sems((n_grp - 1,)), sems((n_grp - 1,)),
                sems((n_blk,)), sems((n_blk,)),
                sems((n_blk,)), sems((n_blk,)),
                sems((n_grp - 1,)), sems((n_grp - 1,)),
            ],
            compiler_params=pltpu.CompilerParams(
                collective_id=0, has_side_effects=True, vmem_limit_bytes=40 * 1024 * 1024
            ),
        )(state, mass.reshape(stars // LANES, LANES), active_index, counts)
        return out, pot.reshape(cap)

    placed = (P(None, ("blk", "grp")), P(("blk", "grp")), P("blk", None), P("blk"))
    return jax.shard_map(
        on_device, mesh=mesh, in_specs=placed, out_specs=(P(None, "blk"), P("blk")), check_vma=False
    )
```

time: 133 us -> 34.8 us (0.26)
  blocking collectives: 57.7 us -> 0 us
  waiting for transfers between devices: 53 us -> 0 us
  Pallas kernels: 0 us -> 29.8 us
  other arithmetic: 11.1 us -> 0 us
  local copies, waits for them, and re-layouts: 6.87 us -> 3.38 us
  starting transfers between devices: 1.92 us -> 0 us
    ppermute x7 -> x0, waiting for transfers between devices: 53 us -> none  [shifted(): return lax.ppermute(block, axis, route)]
    all_gather x1 -> x0, blocking collectives: 52 us -> none  [on_device(): slot_state = lax.all_gather(state, 'grp', axis=1, tiled=True)]
    pallas_call x0 -> x1, Pallas kernels: none -> 29.8 us  [on_device(): pl.pallas_call(functools.partial(kernel, n_blk, n_grp, cap), out_shape=(j...]
    reduce_sum x16 -> x0, other arithmetic: 8.29 us -> none  [the longest x8 5.02 us: pair_terms(): accel = jnp.sum(third[None] * dpos, axis=-1)]
    psum x1 -> x0, blocking collectives: 5.67 us -> none  [on_device(): summed = lax.psum(total, 'grp')]
    gather x1 -> x0, local copies, waits for them, and re-layouts: 3.96 us -> none  [on_device(): active = jnp.take(slot_state, picks, axis=1)]
    mul x8 -> x0, other arithmetic: 2.53 us -> none  [pair_terms(): fifth = 3.0 * along * third * inv * inv]
    ppermute x7 -> x0, starting transfers between devices: 1.92 us -> none  [shifted(): return lax.ppermute(block, axis, route)]
  transfers between devices with their start and end apart: 7 -> 0, of which waited for: 7 -> 0; matrix products, arithmetic and copies ran while one was open for 0% -> 0% of each run, Pallas kernels for 0% -> 0%
where the time goes in v1:
time: 34.8 us; the launch traced here: 34.5 us
  Pallas kernels  29.8 us (86%)
  local copies, waits for them, and re-layouts  3.38 us (10%)
  between operations  1.3 us (4%)
    pallas_call x1, Pallas kernels, on_device(): pl.pallas_call(functools.partial(kernel, n_blk, n_grp, cap), out_shape=(j...  29.8 us
    unnamed x8, local copies, waits for them, and re-layouts  3.38 us

profile of v1, /device:TPU:0, one launch (start us, length us, event | category | flops | bytes accessed | tf_op | source)
XLA Modules:
  0.0 34.5 jit_solution(312905944762104059)
XLA Ops:
  1.3 0.0 copy-start.2
  1.3 0.6 %copy-done.2 = s32[1,32]{1,0:T(1,128)S(1)} copy-done((s32[1,32]{1,0:T(1,128)S(1)}, s32[1,32]{1,0:T(1,128)}, u32[]{:S(2)}) %copy-start.2) | copy-done | bytes 152
  1.9 0.0 copy-start
  1.9 0.9 %copy-done = f32[6,4096]{1,0:T(8,128)S(1)} copy-done((f32[6,4096]{1,0:T(8,128)S(1)}, f32[6,4096]{1,0:T(8,128)}, u32[]{:S(2)}) %copy-start) | copy-done | bytes 98328
  2.8 0.0 copy-start.1
  2.8 0.7 %copy-done.1 = f32[4096]{0:T(1024)S(1)} copy-done((f32[4096]{0:T(1024)S(1)}, f32[4096]{0:T(1024)}, u32[]{:S(2)}) %copy-start.1) | copy-done | bytes 16408
  3.6 29.8 %shard_map.59 = (f32[6,32]{1,0:T(8,128)S(1)}, f32[1,32]{1,0:T(1,128)S(1)}) custom-call(f32[6,4096]{1,0:T(8,128)S(1)} %copy-done, f32[32,128]{1,0:T(8,128)S(1)} %bitcast.2, s32[1,32]{1,0:T(1,128)S(1)} %copy-done.2, s32[1]{0:T(128)S(6)} %copy.8.counts_ref), custom_call_target="tpu_custom_call" | custom-call | tf_op jit(solution)/shard_map/pallas_call | solution.py:175
  33.4 0.6 %copy.9 = f32[6,32]{1,0:T(8,128)} copy(f32[6,32]{1,0:T(8,128)S(1)} %get-tuple-element.8) | data formatting | bytes 1536
  34.0 0.5 %copy.10 = f32[32]{0:T(128)} copy(f32[32]{0:T(128)S(1)} %bitcast.3) | data formatting | bytes 256
Async XLA Ops:
  1.3 0.7 %copy-start.2 = (s32[1,32]{1,0:T(1,128)S(1)}, s32[1,32]{1,0:T(1,128)}, u32[]{:S(2)}) copy-start(s32[1,32]{1,0:T(1,128)} %picks_ref.1) | copy-start | bytes 388
  1.9 0.9 %copy-start = (f32[6,4096]{1,0:T(8,128)S(1)}, f32[6,4096]{1,0:T(8,128)}, u32[]{:S(2)}) copy-start(f32[6,4096]{1,0:T(8,128)} %state_ref.1) | copy-start | bytes 294916
  2.8 0.7 %copy-start.1 = (f32[4096]{0:T(1024)S(1)}, f32[4096]{0:T(1024)}, u32[]{:S(2)}) copy-start(f32[4096]{0:T(1024)} %param.5) | copy-start | bytes 49156

commit v2 on v1

--- a/solution.py
+++ b/solution.py
@@ -10,17 +10,37 @@
 softening = 0.001
 LANES = 128
 MESH = pl.DeviceIdType.MESH
-UNROLL = 4
-
-
-def spread_chunk(state_ref, mass_ref, wide_ref, chunk):
-    start = pl.multiple_of(chunk * LANES, LANES)
-    rows = jnp.concatenate(
-        [state_ref[:, pl.ds(start, LANES)], mass_ref[pl.ds(chunk, 1), :], jnp.zeros((1, LANES), jnp.float32)], axis=0
-    )
-    columns = rows.T
+UNROLL = 8
+SPREAD = 512
+
+
+def pieces(rows):
+    out = []
+    for _ in range(3):
+        piece = rows.astype(jnp.bfloat16).astype(jnp.float32)
+        out.append(piece)
+        rows = rows - piece
+    return jnp.concatenate(out, axis=0)
+
+
+def spread_chunk(state_ref, mass_ref, wide_ref, pick, chunk):
+    parts = []
+    for u in range(SPREAD // LANES):
+        start = pl.multiple_of(chunk * SPREAD + u * LANES, LANES)
+        rows = jnp.concatenate(
+            [
+                state_ref[:, pl.ds(start, LANES)],
+                mass_ref[pl.ds(chunk * (SPREAD // LANES) + u, 1), :],
+                jnp.zeros((1, LANES), jnp.float32),
+            ],
+            axis=0,
+        )
+        parts.append(pieces(rows).T)
+    columns = jnp.concatenate(parts, axis=0).astype(jnp.bfloat16)
+    wide = jnp.dot(columns, pick, preferred_element_type=jnp.float32)
+    at = pl.ds(pl.multiple_of(chunk * SPREAD, SPREAD), SPREAD)
     for c in range(7):
-        wide_ref[c, pl.ds(start, LANES), :] = jnp.broadcast_to(columns[:, c : c + 1], (LANES, LANES))
+        wide_ref[c, at, :] = wide[:, c * LANES : (c + 1) * LANES]
 
 
 def tile_terms(active, wide_ref, stars):
@@ -53,8 +73,8 @@
 
 
 def kernel(
-    n_blk, n_grp, cap, state_ref, mass_ref, picks_ref, counts_ref, out_ref, pot_ref,
-    wide_ref, part_ref, part_in, own_ref, own_in, sum_ref, sum_in, tot_ref, tot_in,
+    n_blk, n_grp, cap, state_in, mass_in, picks_in, counts_in, out_ref, pot_ref,
+    state_ref, mass_ref, picks_ref, counts_ref, load_sem, wide_ref, part_ref, part_in, own_ref, own_in, sum_ref, sum_in, tot_ref, tot_in,
     part_s, part_r, own_s, own_r, sum_s, sum_r, tot_s, tot_r,
 ):
     blk, grp = lax.axis_index("blk"), lax.axis_index("grp")
@@ -73,20 +93,38 @@
     for dt, dr in hops[1:]:
         pl.semaphore_signal(barrier, inc=1, device_id=(slot(dt, dr), grp), device_id_type=MESH)
 
+    loads = [
+        pltpu.make_async_copy(src, dst, load_sem.at[i])
+        for i, (src, dst) in enumerate(
+            [(state_in, state_ref), (mass_in, mass_ref), (picks_in, picks_ref), (counts_in, counts_ref)]
+        )
+    ]
+    for copy in loads:
+        copy.start()
+    for copy in loads:
+        copy.wait()
+
     picks = jnp.concatenate([picks_ref[...] - grp * stars] * size, axis=1)
     lane = lax.broadcasted_iota(jnp.int32, (1, LANES), 1)
     picks = jnp.where(lane // cap == place, picks, -1)
     depth = 512
     row = lax.broadcasted_iota(jnp.int32, (depth, LANES), 0)
-    found = jnp.zeros((6, LANES), jnp.float32)
+    found = jnp.zeros((18, LANES), jnp.float32)
     for k in range(stars // depth):
         hot = jnp.where(row + k * depth == picks, 1.0, 0.0).astype(jnp.bfloat16)
-        rest = state_ref[:, k * depth : (k + 1) * depth]
-        for _ in range(3):
-            piece = rest.astype(jnp.bfloat16)
-            rest = rest - piece.astype(jnp.float32)
-            found = found + jnp.dot(piece, hot, preferred_element_type=jnp.float32)
+        rows = pieces(state_ref[:, k * depth : (k + 1) * depth]).astype(jnp.bfloat16)
+        found = found + jnp.dot(rows, hot, preferred_element_type=jnp.float32)
+    found = found[0:6] + found[6:12] + found[12:18]
     part_ref[...] = jnp.concatenate([found, jnp.zeros((2, LANES), jnp.float32)], axis=0)
+
+    source = lax.broadcasted_iota(jnp.int32, (24, 7 * LANES), 0) % 8
+    target = lax.broadcasted_iota(jnp.int32, (24, 7 * LANES), 1) // LANES
+    pick = jnp.where(source == target, 1.0, 0.0).astype(jnp.bfloat16)
+    chunks = stars // SPREAD
+
+    @pl.loop(0, chunks // 2)
+    def _(chunk):
+        spread_chunk(state_ref, mass_ref, wide_ref, pick, chunk)
 
     pl.semaphore_wait(barrier, n_grp - 1 + n_blk - 1)
 
@@ -100,11 +138,9 @@
     for copy in parts:
         copy.start()
 
-    chunks = stars // LANES
-
-    @pl.loop(0, chunks // 2)
+    @pl.loop(chunks // 2, chunks)
     def _(chunk):
-        spread_chunk(state_ref, mass_ref, wide_ref, chunk)
+        spread_chunk(state_ref, mass_ref, wide_ref, pick, chunk)
 
     own = part_ref[...]
     for d, copy in enumerate(parts):
@@ -119,10 +155,6 @@
             recv_sem=own_r.at[dt * size + dr], device_id=(slot(dt, dr), grp), device_id_type=MESH,
         )
         shares[dt, dr].start()
-
-    @pl.loop(chunks // 2, chunks)
-    def _(chunk):
-        spread_chunk(state_ref, mass_ref, wide_ref, chunk)
 
     results = {}
     for dt in range(tiles):
@@ -175,9 +207,14 @@
         out, pot = pl.pallas_call(
             functools.partial(kernel, n_blk, n_grp, cap),
             out_shape=(jax.ShapeDtypeStruct((6, cap), f32), jax.ShapeDtypeStruct((1, cap), f32)),
-            in_specs=[vmem, vmem, vmem, pl.BlockSpec(memory_space=pltpu.SMEM)],
+            in_specs=[pl.BlockSpec(memory_space=pltpu.HBM)] * 4,
             out_specs=(vmem, vmem),
             scratch_shapes=[
+                pltpu.VMEM((6, stars), f32),
+                pltpu.VMEM((stars // LANES, LANES), f32),
+                pltpu.VMEM((1, cap), jnp.int32),
+                pltpu.SMEM((1,), jnp.int32),
+                sems((4,)),
                 pltpu.VMEM((7, stars, LANES), f32),
                 pltpu.VMEM(tile, f32),
                 pltpu.VMEM((n_grp - 1, *tile), f32),
@@ -193,7 +230,7 @@
                 sems((n_grp - 1,)), sems((n_grp - 1,)),
             ],
             compiler_params=pltpu.CompilerParams(
-                collective_id=0, has_side_effects=True, vmem_limit_bytes=40 * 1024 * 1024
+                collective_id=0, has_side_effects=True, vmem_limit_bytes=67043328
             ),
         )(state, mass.reshape(stars // LANES, LANES), active_index, counts)
         return out, pot.reshape(cap)

time: 34.8 us -> 29.7 us (0.85)
  Pallas kernels: 29.8 us -> 26.4 us
  local copies, waits for them, and re-layouts: 3.38 us -> 1.82 us
    pallas_call x1, Pallas kernels: 29.8 us -> 26.4 us  [on_device(): pl.pallas_call(functools.partial(kernel, n_blk, n_grp, cap), out_shape=(j...]
    unnamed x8 -> x6, local copies, waits for them, and re-layouts: 3.38 us -> 1.82 us
where the time goes in v2:
time: 29.7 us; the launch traced here: 29.5 us
  Pallas kernels  26.4 us (89%)
  local copies, waits for them, and re-layouts  1.82 us (6%)
  between operations  1.29 us (4%)
    pallas_call x1, Pallas kernels, on_device(): pl.pallas_call(functools.partial(kernel, n_blk, n_grp, cap), out_shape=(j...  26.4 us
    unnamed x6, local copies, waits for them, and re-layouts  1.82 us

profile of v2, /device:TPU:0, one launch (start us, length us, event | category | flops | bytes accessed | tf_op | source)
XLA Modules:
  0.0 29.5 jit_solution(8542072327059991594)
XLA Ops:
  1.3 26.4 %shard_map.59 = (f32[6,32]{1,0:T(8,128)}, f32[1,32]{1,0:T(1,128)}) custom-call(f32[6,4096]{1,0:T(8,128)} %state_in.1, f32[32,128]{1,0:T(8,128)} %bitcast.2, s32[1,32]{1,0:T(1,128)} %picks_in.1, s32[1]{0:T(128)S(6)} %copy.8.counts_in), custom_call_target="tpu_custom_call" | custom-call | tf_op jit(solution)/shard_map/pallas_call | solution.py:207
  27.7 0.0 copy-start
  27.7 0.7 %copy-done = f32[6,32]{1,0:T(8,128)S(1)} copy-done((f32[6,32]{1,0:T(8,128)S(1)}, f32[6,32]{1,0:T(8,128)}, u32[]{:S(2)}) %copy-start) | copy-done | bytes 792
  28.4 0.0 copy-start.1
  28.4 0.6 %copy.9 = f32[6,32]{1,0:T(8,128)} copy(f32[6,32]{1,0:T(8,128)S(1)} %copy-done) | data formatting | bytes 1536
  28.9 0.0 copy-done.1
  29.0 0.5 %copy.10 = f32[32]{0:T(128)} copy(f32[32]{0:T(128)S(1)} %bitcast.3) | data formatting | bytes 256
Async XLA Ops:
  27.7 0.7 %copy-start = (f32[6,32]{1,0:T(8,128)S(1)}, f32[6,32]{1,0:T(8,128)}, u32[]{:S(2)}) copy-start(f32[6,32]{1,0:T(8,128)} %get-tuple-element.8) | copy-start | bytes 2308
  28.4 0.6 %copy-start.1 = (f32[1,32]{1,0:T(1,128)S(1)}, f32[1,32]{1,0:T(1,128)}, u32[]{:S(2)}) copy-start(f32[1,32]{1,0:T(1,128)} %get-tuple-element.5) | copy-start | bytes 388

commit v3 on v2

--- a/solution.py
+++ b/solution.py
@@ -73,8 +73,8 @@
 
 
 def kernel(
-    n_blk, n_grp, cap, state_in, mass_in, picks_in, counts_in, out_ref, pot_ref,
-    state_ref, mass_ref, picks_ref, counts_ref, load_sem, wide_ref, part_ref, part_in, own_ref, own_in, sum_ref, sum_in, tot_ref, tot_in,
+    n_blk, n_grp, cap, state_in, mass_in, picks_in, counts_ref, out_ref, pot_ref,
+    state_ref, mass_ref, picks_ref, load_sem, wide_ref, part_ref, part_in, own_ref, own_in, sum_ref, sum_in, tot_ref, tot_in,
     part_s, part_r, own_s, own_r, sum_s, sum_r, tot_s, tot_r,
 ):
     blk, grp = lax.axis_index("blk"), lax.axis_index("grp")
@@ -96,7 +96,7 @@
     loads = [
         pltpu.make_async_copy(src, dst, load_sem.at[i])
         for i, (src, dst) in enumerate(
-            [(state_in, state_ref), (mass_in, mass_ref), (picks_in, picks_ref), (counts_in, counts_ref)]
+            [(state_in, state_ref), (mass_in, mass_ref), (picks_in, picks_ref)]
         )
     ]
     for copy in loads:
@@ -207,14 +207,13 @@
         out, pot = pl.pallas_call(
             functools.partial(kernel, n_blk, n_grp, cap),
             out_shape=(jax.ShapeDtypeStruct((6, cap), f32), jax.ShapeDtypeStruct((1, cap), f32)),
-            in_specs=[pl.BlockSpec(memory_space=pltpu.HBM)] * 4,
+            in_specs=[pl.BlockSpec(memory_space=pltpu.HBM)] * 3 + [pl.BlockSpec(memory_space=pltpu.SMEM)],
             out_specs=(vmem, vmem),
             scratch_shapes=[
                 pltpu.VMEM((6, stars), f32),
                 pltpu.VMEM((stars // LANES, LANES), f32),
                 pltpu.VMEM((1, cap), jnp.int32),
-                pltpu.SMEM((1,), jnp.int32),
-                sems((4,)),
+                sems((3,)),
                 pltpu.VMEM((7, stars, LANES), f32),
                 pltpu.VMEM(tile, f32),
                 pltpu.VMEM((n_grp - 1, *tile), f32),
@@ -230,9 +229,12 @@
                 sems((n_grp - 1,)), sems((n_grp - 1,)),
             ],
             compiler_params=pltpu.CompilerParams(
-                collective_id=0, has_side_effects=True, vmem_limit_bytes=67043328
+                collective_id=0, has_side_effects=True, vmem_limit_bytes=40 * 1024 * 1024
             ),
-        )(state, mass.reshape(stars // LANES, LANES), active_index, counts)
+        )(*(
+            pltpu.with_memory_space_constraint(x, pltpu.HBM)
+            for x in (state, mass.reshape(stars // LANES, LANES), active_index)
+        ), counts)
         return out, pot.reshape(cap)
 
     placed = (P(None, ("blk", "grp")), P(("blk", "grp")), P("blk", None), P("blk"))

time: 29.7 us -> 28.3 us (0.953)
  local copies, waits for them, and re-layouts: 1.82 us -> 1.11 us
  Pallas kernels: 26.4 us -> 25.8 us
    unnamed x6 -> x2, local copies, waits for them, and re-layouts: 1.82 us -> 1.11 us
    pallas_call x1, Pallas kernels: 26.4 us -> 25.8 us  [on_device(): pl.pallas_call(functools.partial(kernel, n_blk, n_grp, cap), out_shape=(j...]
where the time goes in v3:
time: 28.3 us; the launch traced here: 28.2 us
  Pallas kernels  25.8 us (91%)
  between operations  1.29 us (5%)
  local copies, waits for them, and re-layouts  1.11 us (4%)
    pallas_call x1, Pallas kernels, on_device(): pl.pallas_call(functools.partial(kernel, n_blk, n_grp, cap), out_shape=(j...  25.8 us
    unnamed x2, local copies, waits for them, and re-layouts  1.11 us

profile of v3, /device:TPU:0, one launch (start us, length us, event | category | flops | bytes accessed | tf_op | source)
XLA Modules:
  0.0 28.2 jit_solution(17940846166832406586)
XLA Ops:
  1.3 25.8 %shard_map.59 = (f32[6,32]{1,0:T(8,128)S(1)}, f32[1,32]{1,0:T(1,128)S(1)}) custom-call(f32[6,4096]{1,0:T(8,128)} %state_in.1, f32[32,128]{1,0:T(8,128)} %bitcast.3, s32[1,32]{1,0:T(1,128)} %picks_in.1, s32[1]{0:T(128)S(6)} %copy.8.counts_ref), custom_call_target="tpu_custom_call" | custom-call | tf_op jit(solution)/shard_map/pallas_call | solution.py:207
  27.1 0.6 %copy.9 = f32[6,32]{1,0:T(8,128)} copy(f32[6,32]{1,0:T(8,128)S(1)} %get-tuple-element.8) | data formatting | bytes 1536
  27.7 0.5 %copy.10 = f32[32]{0:T(128)} copy(f32[32]{0:T(128)S(1)} %bitcast.2) | data formatting | bytes 256

commit v4 on v3

v4 whole, which is shorter than its diff:
```python
import functools

import jax
import jax.numpy as jnp
from jax import lax
from jax.experimental import pallas as pl
from jax.experimental.pallas import tpu as pltpu
from jax.sharding import PartitionSpec as P

softening = 0.001
LANES = 128
MESH = pl.DeviceIdType.MESH
UNROLL = 8
SPREAD = 512


def pieces(rows):
    out = []
    for _ in range(3):
        piece = rows.astype(jnp.bfloat16).astype(jnp.float32)
        out.append(piece)
        rows = rows - piece
    return jnp.concatenate(out, axis=0)


def spread_chunk(state_ref, mass_ref, wide_ref, pick, chunk):
    parts = []
    for u in range(SPREAD // LANES):
        start = pl.multiple_of(chunk * SPREAD + u * LANES, LANES)
        rows = jnp.concatenate(
            [
                state_ref[:, pl.ds(start, LANES)],
                mass_ref[pl.ds(chunk * (SPREAD // LANES) + u, 1), :],
                jnp.zeros((1, LANES), jnp.float32),
            ],
            axis=0,
        )
        parts.append(pieces(rows).T)
    columns = jnp.concatenate(parts, axis=0).astype(jnp.bfloat16)
    wide = jnp.dot(columns, pick, preferred_element_type=jnp.float32)
    at = pl.ds(pl.multiple_of(chunk * SPREAD, SPREAD), SPREAD)
    for c in range(7):
        wide_ref[c, at, :] = wide[:, c * LANES : (c + 1) * LANES]


def turned(x, cap):
    return [x] + [pltpu.roll(x, k * cap, 1) for k in range(1, LANES // cap)]


def by_block(rows, cap):
    block = lax.broadcasted_iota(jnp.int32, rows[0].shape, 1) // cap
    out = rows[0]
    for b in range(1, len(rows)):
        out = jnp.where(block == b, rows[b], out)
    return out


def tile_terms(packed, wide_ref, stars, cap):
    size = LANES // cap
    high = 8 // size
    moved = turned(packed, cap)
    mine = []
    for c in range(6):
        rows = [moved[(b - c % size) % size][b * high + c // size :][:1] for b in range(size)]
        mine.append(jnp.broadcast_to(by_block(rows, cap), (8, LANES)))

    def body(step, totals):
        totals = list(totals)
        for u in range(UNROLL):
            at = pl.ds(pl.multiple_of((step * UNROLL + u) * 8, 8), 8)
            dx = [wide_ref[c, at, :] - mine[c] for c in range(3)]
            dv = [wide_ref[c, at, :] - mine[c] for c in range(3, 6)]
            raw = dx[0] * dx[0] + dx[1] * dx[1] + dx[2] * dx[2]
            weight = jnp.where(raw == 0.0, 0.0, wide_ref[6, at, :])
            inv = lax.rsqrt(raw + softening)
            square = inv * inv
            first = weight * inv
            third = first * square
            along = dx[0] * dv[0] + dx[1] * dv[1] + dx[2] * dv[2]
            ratio = (3.0 * along) * square
            for c in range(3):
                totals[c] = totals[c] + third * dx[c]
                totals[3 + c] = totals[3 + c] + third * (dv[c] - ratio * dx[c])
            totals[6] = totals[6] + first
        return tuple(totals)

    zero = jnp.zeros((8, LANES), jnp.float32)
    totals = lax.fori_loop(0, stars // (8 * UNROLL), body, (zero,) * 7)
    sums = [jnp.sum(t, axis=0, keepdims=True) for t in totals]
    moved = turned(jnp.concatenate(sums[:6] + [-sums[6], jnp.zeros((1, LANES), jnp.float32)], axis=0), cap)
    rows = []
    for b in range(size):
        for r in range(high):
            rows.append(by_block([moved[(q - b) % size][r * size + q :][:1] for q in range(size)], cap))
    return jnp.concatenate(rows, axis=0)


def kernel(
    n_blk, n_grp, cap, state_in, mass_in, picks_in, counts_ref, out_ref, pot_ref,
    state_ref, mass_ref, picks_ref, load_sem, wide_ref, part_ref, own_in, sum_ref, sum_in,
    own_s, own_r, sum_s, sum_r,
):
    blk, grp = lax.axis_index("blk"), lax.axis_index("grp")
    stars = state_ref.shape[1]
    size = LANES // cap
    high = 8 // size
    tiles = n_blk // size
    group = size * n_grp
    everyone = n_blk * n_grp
    tile, place = blk // size, blk % size
    me = blk * n_grp + grp

    def ahead(i):
        dt, dr, dg = i // group, (i % group) // n_grp, i % n_grp
        return ((tile + dt) % tiles) * size + (place + dr) % size, (grp + dg) % n_grp

    def behind(i):
        dt, dr, dg = i // group, (i % group) // n_grp, i % n_grp
        return ((tile + tiles - dt) % tiles) * size + (place + size - dr) % size, (grp + n_grp - dg) % n_grp

    barrier = pltpu.get_barrier_semaphore()

    @pl.loop(1, everyone)
    def _(i):
        pl.semaphore_signal(barrier, inc=1, device_id=ahead(everyone - i), device_id_type=MESH)

    loads = [
        pltpu.make_async_copy(src, dst, load_sem.at[i])
        for i, (src, dst) in enumerate(
            [(state_in, state_ref), (mass_in, mass_ref), (picks_in, picks_ref)]
        )
    ]
    for copy in loads:
        copy.start()
    for copy in loads:
        copy.wait()

    picks = jnp.concatenate([picks_ref[...] - grp * stars] * size, axis=1)
    depth = 512
    row = lax.broadcasted_iota(jnp.int32, (depth, LANES), 0)
    found = jnp.zeros((18, LANES), jnp.float32)
    for k in range(stars // depth):
        hot = jnp.where(row + k * depth == picks, 1.0, 0.0).astype(jnp.bfloat16)
        rows = pieces(state_ref[:, k * depth : (k + 1) * depth]).astype(jnp.bfloat16)
        found = found + jnp.dot(rows, hot, preferred_element_type=jnp.float32)
    found = found[0:6] + found[6:12] + found[12:18]
    found = jnp.concatenate([found, jnp.zeros((2, LANES), jnp.float32)], axis=0)
    part = jnp.concatenate(
        [by_block([found[r * size + q :][:1] for q in range(size)], cap) for r in range(high)], axis=0
    )
    part_ref[...] = part

    source = lax.broadcasted_iota(jnp.int32, (24, 7 * LANES), 0) % 8
    target = lax.broadcasted_iota(jnp.int32, (24, 7 * LANES), 1) // LANES
    pick = jnp.where(source == target, 1.0, 0.0).astype(jnp.bfloat16)
    chunks = stars // SPREAD

    @pl.loop(0, chunks // 2)
    def _(chunk):
        spread_chunk(state_ref, mass_ref, wide_ref, pick, chunk)

    pl.semaphore_wait(barrier, everyone - 1)

    def share(i):
        return pltpu.make_async_remote_copy(
            src_ref=part_ref, dst_ref=own_in.at[i], send_sem=own_s.at[i], recv_sem=own_r.at[i],
            device_id=ahead(i), device_id_type=MESH,
        )

    def give(i):
        return pltpu.make_async_remote_copy(
            src_ref=sum_ref.at[i // group, (i % group) // n_grp], dst_ref=sum_in.at[me], send_sem=sum_s.at[i],
            recv_sem=sum_r.at[me], device_id=behind(i), device_id_type=MESH,
        )

    def take(i):
        there = behind(i)
        at = there[0] * n_grp + there[1]
        return pltpu.make_async_remote_copy(
            src_ref=part_ref, dst_ref=sum_in.at[at], send_sem=sum_s.at[i], recv_sem=sum_r.at[at],
            device_id=there, device_id_type=MESH,
        )

    @pl.loop(1, everyone)
    def _(i):
        share(i).start()

    @pl.loop(chunks // 2, chunks)
    def _(chunk):
        spread_chunk(state_ref, mass_ref, wide_ref, pick, chunk)

    for dt in range(tiles):
        first = dt * group + (dt == 0)

        @pl.loop(first, (dt + 1) * group)
        def _(i):
            share(i).wait_recv()

        packed = []
        for dr in range(size):
            slot = part if dt == 0 and dr == 0 else own_in[dt * group + dr * n_grp]
            for dg in range(1, n_grp):
                slot = slot + own_in[dt * group + dr * n_grp + dg]
            packed.append(slot)
        terms = tile_terms(jnp.concatenate(packed, axis=0), wide_ref, stars, cap)
        for dr in range(size):
            sum_ref[dt, dr] = terms[dr * high : (dr + 1) * high]
        if dt == 0:
            sum_in[me] = terms[:high]

        @pl.loop(first, (dt + 1) * group)
        def _(i):
            give(i).start()

    @pl.loop(1, everyone)
    def _(i):
        take(i).wait_recv()

    total = sum_in[0]
    for k in range(1, everyone):
        total = total + sum_in[k]
    moved = turned(total, cap)
    rows = [moved[(size - c % size) % size][c // size :][:1, :cap] for c in range(7)]
    live = lax.broadcasted_iota(jnp.int32, (1, cap), 1) < counts_ref[0]
    out_ref[...] = jnp.where(live, jnp.concatenate(rows[:6], axis=0), 0.0)
    pot_ref[...] = jnp.where(live, rows[6], 0.0)

    @pl.loop(1, everyone)
    def _(i):
        share(i).wait_send()
        give(i).wait_send()


def solution(mesh):
    n_blk, n_grp = mesh.shape["blk"], mesh.shape["grp"]

    def on_device(state, mass, active_index, counts):
        stars, cap = state.shape[1], active_index.shape[1]
        f32 = jnp.float32
        tile = (8 * cap // LANES, LANES)
        everyone = n_blk * n_grp
        sems = pltpu.SemaphoreType.DMA
        vmem = pl.BlockSpec(memory_space=pltpu.VMEM)
        out, pot = pl.pallas_call(
            functools.partial(kernel, n_blk, n_grp, cap),
            out_shape=(jax.ShapeDtypeStruct((6, cap), f32), jax.ShapeDtypeStruct((1, cap), f32)),
            in_specs=[pl.BlockSpec(memory_space=pltpu.HBM)] * 3 + [pl.BlockSpec(memory_space=pltpu.SMEM)],
            out_specs=(vmem, vmem),
            scratch_shapes=[
                pltpu.VMEM((6, stars), f32),
                pltpu.VMEM((stars // LANES, LANES), f32),
                pltpu.VMEM((1, cap), jnp.int32),
                sems((3,)),
                pltpu.VMEM((7, stars, LANES), f32),
                pltpu.VMEM(tile, f32),
                pltpu.VMEM((everyone, *tile), f32),
                pltpu.VMEM((n_blk * cap // LANES, LANES // cap, *tile), f32),
                pltpu.VMEM((everyone, *tile), f32),
                sems((everyone,)), sems((everyone,)), sems((everyone,)), sems((everyone,)),
            ],
            compiler_params=pltpu.CompilerParams(
                collective_id=0, has_side_effects=True, vmem_limit_bytes=40 * 1024 * 1024
            ),
        )(*(
            pltpu.with_memory_space_constraint(x, pltpu.HBM)
            for x in (state, mass.reshape(stars // LANES, LANES), active_index)
        ), counts)
        return out, pot.reshape(cap)

    placed = (P(None, ("blk", "grp")), P(("blk", "grp")), P("blk", None), P("blk"))
    return jax.shard_map(
        on_device, mesh=mesh, in_specs=placed, out_specs=(P(None, "blk"), P("blk")), check_vma=False
    )
```

time: 28.3 us -> 27.5 us (0.972)
  Pallas kernels: 25.8 us -> 25 us
    pallas_call x1, Pallas kernels: 25.8 us -> 25 us  [on_device(): pl.pallas_call(functools.partial(kernel, n_blk, n_grp, cap), out_shape=(j...]
where the time goes in v4:
time: 27.5 us; the launch traced here: 27.4 us
  Pallas kernels  25 us (91%)
  between operations  1.29 us (5%)
  local copies, waits for them, and re-layouts  1.11 us (4%)
    pallas_call x1, Pallas kernels, on_device(): pl.pallas_call(functools.partial(kernel, n_blk, n_grp, cap), out_shape=(j...  25 us
    unnamed x2, local copies, waits for them, and re-layouts  1.11 us

profile of v4, /device:TPU:0, one launch (start us, length us, event | category | flops | bytes accessed | tf_op | source)
XLA Modules:
  0.0 27.4 jit_solution(16894309135523683600)
XLA Ops:
  1.3 25.0 %shard_map.59 = (f32[6,32]{1,0:T(8,128)S(1)}, f32[1,32]{1,0:T(1,128)S(1)}) custom-call(f32[6,4096]{1,0:T(8,128)} %state_in.1, f32[32,128]{1,0:T(8,128)} %bitcast.3, s32[1,32]{1,0:T(1,128)} %picks_in.1, s32[1]{0:T(128)S(6)} %copy.8.counts_ref), custom_call_target="tpu_custom_call" | custom-call | tf_op jit(solution)/shard_map/pallas_call | solution.py:244
  26.3 0.6 %copy.9 = f32[6,32]{1,0:T(8,128)} copy(f32[6,32]{1,0:T(8,128)S(1)} %get-tuple-element.8) | data formatting | bytes 1536
  26.8 0.5 %copy.10 = f32[32]{0:T(128)} copy(f32[32]{0:T(128)S(1)} %bitcast.2) | data formatting | bytes 256

commit v5 on v4

--- a/solution.py
+++ b/solution.py
@@ -97,8 +97,8 @@
 
 def kernel(
     n_blk, n_grp, cap, state_in, mass_in, picks_in, counts_ref, out_ref, pot_ref,
-    state_ref, mass_ref, picks_ref, load_sem, wide_ref, part_ref, own_in, sum_ref, sum_in,
-    own_s, own_r, sum_s, sum_r,
+    state_ref, mass_ref, picks_ref, load_sem, wide_ref, part_ref, own_in, list_ref, list_in, sum_ref, sum_in,
+    own_s, own_r, list_s, list_r, sum_s, sum_r,
 ):
     blk, grp = lax.axis_index("blk"), lax.axis_index("grp")
     stars = state_ref.shape[1]
@@ -120,9 +120,12 @@
 
     barrier = pltpu.get_barrier_semaphore()
 
-    @pl.loop(1, everyone)
-    def _(i):
-        pl.semaphore_signal(barrier, inc=1, device_id=ahead(everyone - i), device_id_type=MESH)
+    for dt in range(1, tiles):
+        pl.semaphore_signal(barrier, inc=1, device_id=ahead(dt * group), device_id_type=MESH)
+
+    @pl.loop(1, group)
+    def _(i):
+        pl.semaphore_signal(barrier, inc=1, device_id=ahead(group - i), device_id_type=MESH)
 
     loads = [
         pltpu.make_async_copy(src, dst, load_sem.at[i])
@@ -159,12 +162,18 @@
     def _(chunk):
         spread_chunk(state_ref, mass_ref, wide_ref, pick, chunk)
 
-    pl.semaphore_wait(barrier, everyone - 1)
+    pl.semaphore_wait(barrier, group - 1 + tiles - 1)
 
     def share(i):
         return pltpu.make_async_remote_copy(
             src_ref=part_ref, dst_ref=own_in.at[i], send_sem=own_s.at[i], recv_sem=own_r.at[i],
             device_id=ahead(i), device_id_type=MESH,
+        )
+
+    def pass_on(dt):
+        return pltpu.make_async_remote_copy(
+            src_ref=list_ref, dst_ref=list_in.at[dt], send_sem=list_s.at[dt], recv_sem=list_r.at[dt],
+            device_id=ahead(dt * group), device_id_type=MESH,
         )
 
     def give(i):
@@ -181,7 +190,7 @@
             device_id=there, device_id_type=MESH,
         )
 
-    @pl.loop(1, everyone)
+    @pl.loop(1, group)
     def _(i):
         share(i).start()
 
@@ -189,20 +198,27 @@
     def _(chunk):
         spread_chunk(state_ref, mass_ref, wide_ref, pick, chunk)
 
+    @pl.loop(1, group)
+    def _(i):
+        share(i).wait_recv()
+
+    packed = []
+    for dr in range(size):
+        slot = part if dr == 0 else own_in[dr * n_grp]
+        for dg in range(1, n_grp):
+            slot = slot + own_in[dr * n_grp + dg]
+        packed.append(slot)
+    packed = jnp.concatenate(packed, axis=0)
+    list_ref[...] = packed
+    for dt in range(1, tiles):
+        pass_on(dt).start()
+
     for dt in range(tiles):
         first = dt * group + (dt == 0)
-
-        @pl.loop(first, (dt + 1) * group)
-        def _(i):
-            share(i).wait_recv()
-
-        packed = []
-        for dr in range(size):
-            slot = part if dt == 0 and dr == 0 else own_in[dt * group + dr * n_grp]
-            for dg in range(1, n_grp):
-                slot = slot + own_in[dt * group + dr * n_grp + dg]
-            packed.append(slot)
-        terms = tile_terms(jnp.concatenate(packed, axis=0), wide_ref, stars, cap)
+        if dt > 0:
+            pass_on(dt).wait_recv()
+            packed = list_in[dt]
+        terms = tile_terms(packed, wide_ref, stars, cap)
         for dr in range(size):
             sum_ref[dt, dr] = terms[dr * high : (dr + 1) * high]
         if dt == 0:
@@ -227,8 +243,14 @@
 
     @pl.loop(1, everyone)
     def _(i):
+        give(i).wait_send()
+
+    @pl.loop(1, group)
+    def _(i):
         share(i).wait_send()
-        give(i).wait_send()
+
+    for dt in range(1, tiles):
+        pass_on(dt).wait_send()
 
 
 def solution(mesh):
@@ -238,6 +260,8 @@
         stars, cap = state.shape[1], active_index.shape[1]
         f32 = jnp.float32
         tile = (8 * cap // LANES, LANES)
+        tiles = n_blk * cap // LANES
+        near = n_grp * LANES // cap
         everyone = n_blk * n_grp
         sems = pltpu.SemaphoreType.DMA
         vmem = pl.BlockSpec(memory_space=pltpu.VMEM)
@@ -253,10 +277,12 @@
                 sems((3,)),
                 pltpu.VMEM((7, stars, LANES), f32),
                 pltpu.VMEM(tile, f32),
+                pltpu.VMEM((near, *tile), f32),
+                pltpu.VMEM((8, LANES), f32),
+                pltpu.VMEM((tiles, 8, LANES), f32),
+                pltpu.VMEM((tiles, LANES // cap, *tile), f32),
                 pltpu.VMEM((everyone, *tile), f32),
-                pltpu.VMEM((n_blk * cap // LANES, LANES // cap, *tile), f32),
-                pltpu.VMEM((everyone, *tile), f32),
-                sems((everyone,)), sems((everyone,)), sems((everyone,)), sems((everyone,)),
+                sems((near,)), sems((near,)), sems((tiles,)), sems((tiles,)), sems((everyone,)), sems((everyone,)),
             ],
             compiler_params=pltpu.CompilerParams(
                 collective_id=0, has_side_effects=True, vmem_limit_bytes=40 * 1024 * 1024

time: 27.5 us -> 26.3 us (0.956)
  Pallas kernels: 25 us -> 23.7 us
    pallas_call x1, Pallas kernels: 25 us -> 23.7 us  [on_device(): pl.pallas_call(functools.partial(kernel, n_blk, n_grp, cap), out_shape=(j...]
where the time goes in v5:
time: 26.3 us; the launch traced here: 26.1 us
  Pallas kernels  23.7 us (90%)
  between operations  1.29 us (5%)
  local copies, waits for them, and re-layouts  1.11 us (4%)
    pallas_call x1, Pallas kernels, on_device(): pl.pallas_call(functools.partial(kernel, n_blk, n_grp, cap), out_shape=(j...  23.7 us
    unnamed x2, local copies, waits for them, and re-layouts  1.11 us

profile of v5, /device:TPU:0, one launch (start us, length us, event | category | flops | bytes accessed | tf_op | source)
XLA Modules:
  0.0 26.1 jit_solution(3969557049515711424)
XLA Ops:
  1.3 23.7 %shard_map.59 = (f32[6,32]{1,0:T(8,128)S(1)}, f32[1,32]{1,0:T(1,128)S(1)}) custom-call(f32[6,4096]{1,0:T(8,128)} %state_in.1, f32[32,128]{1,0:T(8,128)} %bitcast.3, s32[1,32]{1,0:T(1,128)} %picks_in.1, s32[1]{0:T(128)S(6)} %copy.8.counts_ref), custom_call_target="tpu_custom_call" | custom-call | tf_op jit(solution)/shard_map/pallas_call | solution.py:268
  25.0 0.6 %copy.9 = f32[6,32]{1,0:T(8,128)} copy(f32[6,32]{1,0:T(8,128)S(1)} %get-tuple-element.8) | data formatting | bytes 1536
  25.6 0.5 %copy.10 = f32[32]{0:T(128)} copy(f32[32]{0:T(128)S(1)} %bitcast.2) | data formatting | bytes 256

commit v6 on v5

--- a/solution.py
+++ b/solution.py
@@ -55,7 +55,7 @@
     return out
 
 
-def tile_terms(packed, wide_ref, stars, cap):
+def tile_terms(packed, wide_ref, begin, end, cap):
     size = LANES // cap
     high = 8 // size
     moved = turned(packed, cap)
@@ -85,7 +85,7 @@
         return tuple(totals)
 
     zero = jnp.zeros((8, LANES), jnp.float32)
-    totals = lax.fori_loop(0, stars // (8 * UNROLL), body, (zero,) * 7)
+    totals = lax.fori_loop(begin // (8 * UNROLL), end // (8 * UNROLL), body, (zero,) * 7)
     sums = [jnp.sum(t, axis=0, keepdims=True) for t in totals]
     moved = turned(jnp.concatenate(sums[:6] + [-sums[6], jnp.zeros((1, LANES), jnp.float32)], axis=0), cap)
     rows = []
@@ -93,6 +93,14 @@
         for r in range(high):
             rows.append(by_block([moved[(q - b) % size][r * size + q :][:1] for q in range(size)], cap))
     return jnp.concatenate(rows, axis=0)
+
+
+def each(first, last, do):
+    if last - first <= 32:
+        for i in range(first, last):
+            do(i)
+    else:
+        pl.loop(first, last)(do)
 
 
 def kernel(
@@ -190,17 +198,13 @@
             device_id=there, device_id_type=MESH,
         )
 
-    @pl.loop(1, group)
-    def _(i):
-        share(i).start()
+    each(1, group, lambda i: share(i).start())
 
     @pl.loop(chunks // 2, chunks)
     def _(chunk):
         spread_chunk(state_ref, mass_ref, wide_ref, pick, chunk)
 
-    @pl.loop(1, group)
-    def _(i):
-        share(i).wait_recv()
+    each(1, group, lambda i: share(i).wait_recv())
 
     packed = []
     for dr in range(size):
@@ -213,24 +217,22 @@
     for dt in range(1, tiles):
         pass_on(dt).start()
 
-    for dt in range(tiles):
-        first = dt * group + (dt == 0)
-        if dt > 0:
-            pass_on(dt).wait_recv()
-            packed = list_in[dt]
-        terms = tile_terms(packed, wide_ref, stars, cap)
+    def hand_out(dt, terms):
         for dr in range(size):
             sum_ref[dt, dr] = terms[dr * high : (dr + 1) * high]
-        if dt == 0:
-            sum_in[me] = terms[:high]
-
-        @pl.loop(first, (dt + 1) * group)
-        def _(i):
-            give(i).start()
-
-    @pl.loop(1, everyone)
-    def _(i):
-        take(i).wait_recv()
+
+        each(dt * group + (dt == 0), (dt + 1) * group, lambda i: give(i).start())
+
+    most = stars // 4 * 3
+    terms = tile_terms(packed, wide_ref, 0, most, cap)
+    for dt in range(1, tiles):
+        pass_on(dt).wait_recv()
+        hand_out(dt, tile_terms(list_in[dt], wide_ref, 0, stars, cap))
+    terms = terms + tile_terms(packed, wide_ref, most, stars, cap)
+    sum_in[me] = terms[:high]
+    hand_out(0, terms)
+
+    each(1, everyone, lambda i: take(i).wait_recv())
 
     total = sum_in[0]
     for k in range(1, everyone):
@@ -241,13 +243,9 @@
     out_ref[...] = jnp.where(live, jnp.concatenate(rows[:6], axis=0), 0.0)
     pot_ref[...] = jnp.where(live, rows[6], 0.0)
 
-    @pl.loop(1, everyone)
-    def _(i):
-        give(i).wait_send()
-
-    @pl.loop(1, group)
-    def _(i):
-        share(i).wait_send()
+    each(1, everyone, lambda i: give(i).wait_send())
+
+    each(1, group, lambda i: share(i).wait_send())
 
     for dt in range(1, tiles):
         pass_on(dt).wait_send()

time: 26.3 us -> 24.7 us (0.939)
  Pallas kernels: 23.7 us -> 22.2 us
    pallas_call x1, Pallas kernels: 23.7 us -> 22.2 us  [on_device(): pl.pallas_call(functools.partial(kernel, n_blk, n_grp, cap), out_shape=(j...]
where the time goes in v6:
time: 24.7 us; the launch traced here: 24.6 us
  Pallas kernels  22.2 us (90%)
  between operations  1.29 us (5%)
  local copies, waits for them, and re-layouts  1.11 us (4%)
    pallas_call x1, Pallas kernels, on_device(): pl.pallas_call(functools.partial(kernel, n_blk, n_grp, cap), out_shape=(j...  22.2 us
    unnamed x2, local copies, waits for them, and re-layouts  1.11 us

profile of v6, /device:TPU:0, one launch (start us, length us, event | category | flops | bytes accessed | tf_op | source)
XLA Modules:
  0.0 24.6 jit_solution(16289062796856784243)
XLA Ops:
  1.3 22.2 %shard_map.59 = (f32[6,32]{1,0:T(8,128)S(1)}, f32[1,32]{1,0:T(1,128)S(1)}) custom-call(f32[6,4096]{1,0:T(8,128)} %state_in.1, f32[32,128]{1,0:T(8,128)} %bitcast.3, s32[1,32]{1,0:T(1,128)} %picks_in.1, s32[1]{0:T(128)S(6)} %copy.8.counts_ref), custom_call_target="tpu_custom_call" | custom-call | tf_op jit(solution)/shard_map/pallas_call | solution.py:266
  23.5 0.6 %copy.9 = f32[6,32]{1,0:T(8,128)} copy(f32[6,32]{1,0:T(8,128)S(1)} %get-tuple-element.8) | data formatting | bytes 1536
  24.1 0.5 %copy.10 = f32[32]{0:T(128)} copy(f32[32]{0:T(128)S(1)} %bitcast.2) | data formatting | bytes 256
